TPU v7x, 32 devices: a whole 2x2x4 slice. The times are simulated.
32 devices in a mesh: cell: 2 (over y), gene: 16 (over z, x, core).
Axes of the slice: x: 2, y: 2, z: 4, core: 2. Of those that a mesh axis runs over, the one named last changes fastest.
Arguments:
- blocks: bfloat16 [1536, 256, 256], P(('cell', 'gene')), may hold values from 0 to 255, as said below
- block_rows: int32 [1536], P(('cell', 'gene')), may hold values from 0 to 15, as said below
- block_cols: int32 [1536], P(('cell', 'gene')), may hold values from 0 to 3, as said below
- block_count: int32 [32], P(('cell', 'gene')), may hold values from 2 to 48, as said below
- cell_factor: float32 [8192, 128], P(('cell', 'gene')), as said below
- gene_factor: float32 [16384, 128], P('gene'), as said below
Outputs:
- cell_new: float32 [8192, 128], P(('cell', 'gene'))
- gene_new: float32 [16384, 128], P('gene')
Inputs may be any that keep to these rules, and one draw needn't show every extreme that they name: `blocks`: counts are whole numbers. `block_rows`: within one device the live slots and the padding slots name distinct block positions. `block_cols`: within one device the live slots and the padding slots name distinct block positions. `block_count`: some device has all 48 slots live. `cell_factor`: positive entries. `gene_factor`: positive entries.
All inputs are finite; a program needn't handle non-finite values.
Results may differ from a plain program's by a relative error of at most 0.00084.
Values may be sent and summed in bfloat16 or wider, within the bound.
A program may use at most 64 MiB of HBM per device.

v0:
```python
import functools

import jax
import jax.numpy as jnp
from jax import lax
from jax.experimental import pallas as pl
from jax.experimental.pallas import tpu as pltpu
from jax.sharding import PartitionSpec as P

MESH = pl.DeviceIdType.MESH
F32 = jnp.float32
BF = jnp.bfloat16
I16 = jnp.int16


def digits(group):
    cores = 2
    far = 4
    return far, group // (far * cores), cores


class Spot:
    def __init__(self, group):
        self.group = group
        self.far, self.near, self.cores = digits(group)
        self.me = lax.axis_index("gene")
        self.a = self.me // (self.near * self.cores)
        self.b = lax.rem(self.me // self.cores, self.near)
        self.c = lax.rem(self.me, self.cores)

    def a_at(self, d):
        return lax.rem(self.a + d, self.far)

    def b_at(self, d):
        return lax.rem(self.b + d, self.near)

    def index(self, a, b, c):
        return (a * self.near + b) * self.cores + c


def send(src, dst, send_sem, recv_sem, where):
    copy = pltpu.make_async_remote_copy(
        src_ref=src, dst_ref=dst, send_sem=send_sem, recv_sem=recv_sem,
        device_id=where, device_id_type=MESH,
    )
    copy.start()
    return copy


def greet(axis, size):
    barrier = pltpu.get_barrier_semaphore()
    me = lax.axis_index(axis)
    for d in range(1, size):
        pl.semaphore_signal(
            barrier, inc=1, device_id={axis: lax.rem(me + d, size)}, device_id_type=MESH
        )


def encode(value, code, scale):
    top = jnp.max(jnp.abs(value), axis=0, keepdims=True)
    factor = jnp.where(top > 0.0, 32767.0 / top, 0.0)
    code[...] = jnp.round(value * factor).astype(jnp.int32).astype(jnp.int16)
    scale[...] = top * (1.0 / 32767.0)


def decode(code, scale):
    return code[...].astype(jnp.int32).astype(F32) * scale[...]


def far_order(far):
    order = []
    for step in range(1, far // 2 + 1):
        order.append(step)
        if far - step != step:
            order.append(far - step)
    return order


class Gather:
    def __init__(self, spot, own, out, sems):
        self.spot, self.own, self.out = spot, own, out
        self.zs, self.zr, self.xs, self.xr, self.cs, self.cr = sems
        self.zc, self.xc, self.cc = {}, {}, {}

    def place(self, d, e):
        spot = self.spot
        return self.out.at[spot.index(spot.a_at(d), spot.b_at(e), spot.c)]

    def start(self, order):
        spot = self.spot
        for d in order:
            self.zc[d] = send(self.own, self.out.at[spot.me], self.zs.at[d], self.zr.at[d],
                              {"gene": spot.index(spot.a_at(spot.far - d), spot.b, spot.c)})
        self.forward(0, self.own)

    def forward(self, d, src):
        spot = self.spot
        for e in range(1, spot.near):
            self.xc[d, e] = send(src, self.place(d, 0), self.xs.at[d, e], self.xr.at[d, e],
                                 {"gene": spot.index(spot.a, spot.b_at(spot.near - e), spot.c)})
        self.pair(d, 0, src)

    def pair(self, d, e, src):
        spot = self.spot
        self.cc[d, e] = send(src, self.place(d, e), self.cs.at[d, e], self.cr.at[d, e],
                             {"gene": spot.index(spot.a, spot.b, 1 - spot.c)})

    def take_far(self, d):
        self.zc[d].wait_recv()
        self.forward(d, self.place(d, 0))

    def take_near(self, d):
        for e in range(1, self.spot.near):
            self.xc[d, e].wait_recv()
            self.pair(d, e, self.place(d, e))

    def ready(self, d):
        for e in range(self.spot.near):
            self.cc[d, e].wait_recv()

    def close(self):
        for copy in [*self.zc.values(), *self.xc.values(), *self.cc.values()]:
            copy.wait_send()


def gather_sems(far, near):
    dma = pltpu.SemaphoreType.DMA
    return [dma((far,))] * 2 + [dma((far, near))] * 4


def share(spot, src, parts, ss, sr):
    return [
        send(src, parts.at[spot.me], ss.at[d], sr.at[d], {"gene": lax.rem(spot.me + d, spot.group)})
        for d in range(1, spot.group)
    ]


def step_kernel(group, cells, blocks, table, cell, gene, cell_new, gene_new,
                held, gene_bf, flipped, own_bf, own_sum, parts, cell_bf,
                next_bf, next_sum, next_parts, next_cell, numer, p1, p2, p3, t2, t3,
                p2m, p3m, t2m, t3m, acc, code, codem, other, otherm, group_sum, other_sum, *sems):
    spot = Spot(group)
    far, near = spot.far, spot.near
    a, b, c = spot.a, spot.b, spot.c
    slots, width, _ = blocks.shape
    tiles = gene.shape[0]
    rows = cell.shape[0]
    sub = width // rows
    one_sems, two_sems = sems[0:6], sems[6:12]
    s1, r1, s2, r2, s3, r3, gs, gr, ns, nr, fs, fr, os, orr, ls, u2, v2, u3, v3, uf, vf = sems[12:]
    load = pltpu.make_async_copy(blocks, held.at[pl.ds(0, slots)], ls.at[0])
    load.start()

    greet("gene", group)
    greet("cell", cells)
    held[slots] = jnp.zeros((width, width), BF)
    own_bf[...] = cell[...].astype(BF)
    cell_bf[spot.me] = cell[...].astype(BF)
    pl.semaphore_wait(pltpu.get_barrier_semaphore(), group - 1 + cells - 1)

    order = far_order(far) + [0]
    one = Gather(spot, own_bf, cell_bf, one_sems)
    one.start(order[:-1])
    first_sum = jnp.zeros((1, gene.shape[-1]), F32)
    for j in range(tiles):
        first_sum += jnp.sum(gene[j], axis=0, keepdims=True)
    own_sum[...] = first_sum
    parts[spot.me] = first_sum
    shared = share(spot, own_sum, parts, gs, gr)
    for j in range(tiles):
        gene_bf[j] = gene[j].astype(BF)
        flipped[j] = gene[j].astype(BF).T
    one.take_near(0)
    load.wait()

    def ratio_of(source, g, j):
        rows_bf = source[g]
        slot = table[(g // sub) * tiles + j]
        if sub == 1:
            x = held[slot]
        else:
            x = held[slot, pl.ds(pl.multiple_of(lax.rem(g, sub) * rows, rows), rows), :]
        model = jnp.dot(rows_bf, flipped[j], preferred_element_type=F32)
        return (x.astype(F32) / model).astype(BF), rows_bf

    def first_half(d, core):
        def body(e, carry):
            g = spot.index(spot.a_at(d), spot.b_at(e), core)
            total = None
            for j in range(tiles):
                ratio, _ = ratio_of(cell_bf, g, j)
                term = jnp.dot(ratio, gene_bf[j], preferred_element_type=F32)
                total = term if total is None else total + term
            numer[g] = total
            return carry

        lax.fori_loop(0, near, body, 0)

    c1, c2, c3 = {}, {}, {}

    def stage_one(d):
        for e in [*range(1, near), 0]:
            at = spot.index(spot.a_at(d), spot.b_at(e), 1 - c)
            c1[d, e] = send(numer.at[at], p1.at[d, e], s1.at[d, e], r1.at[d, e],
                            {"gene": spot.index(a, b, 1 - c)})

    def weight(g):
        return jnp.mean(cell_bf[g].astype(F32), axis=1, keepdims=True)

    def stage_two(d):
        for e in range(1, near):
            c1[d, e].wait_recv()
            g = spot.index(spot.a_at(d), spot.b_at(e), c)
            encode((numer[g] + p1[d, e]) * weight(g), t2.at[d, e], t2m.at[d, e])
            where = {"gene": spot.index(a, spot.b_at(e), c)}
            c2[d, e] = (
                send(t2.at[d, e], p2.at[d, e], s2.at[d, e], r2.at[d, e], where),
                send(t2m.at[d, e], p2m.at[d, e], u2.at[d, e], v2.at[d, e], where),
            )

    def summed(d):
        c1[d, 0].wait_recv()
        g = spot.index(spot.a_at(d), b, c)
        value = (numer[g] + p1[d, 0]) * weight(g)
        for e in range(1, near):
            for copy in c2[d, e]:
                copy.wait_recv()
            value += decode(p2.at[d, e], p2m.at[d, e])
        return value

    def stage_three(d):
        encode(summed(d), t3.at[d], t3m.at[d])
        where = {"gene": spot.index(spot.a_at(d), b, c)}
        c3[d] = (
            send(t3.at[d], p3.at[d], s3.at[d], r3.at[d], where),
            send(t3m.at[d], p3m.at[d], u3.at[d], v3.at[d], where),
        )

    one.ready(0)
    first_half(0, 1 - c)
    stage_one(0)
    for i, d in enumerate(order[:-1]):
        one.take_far(d)
        if i == 0:
            continue
        one.take_near(order[i - 1])
    one.take_near(order[-2])
    for i, d in enumerate(order[:-1]):
        one.ready(d)
        first_half(d, 1 - c)
        stage_one(d)
        if i >= 2:
            stage_three(order[i - 2])
        first_half(d, c)
        stage_two(d)
    stage_three(order[-3])
    first_half(0, c)
    stage_two(0)
    stage_three(order[-2])
    for copy in shared:
        copy.wait()
    total = jnp.sum(parts[...], axis=0)
    value = summed(0)
    for d in order[:-1]:
        for copy in c3[d]:
            copy.wait_recv()
        value += decode(p3.at[d], p3m.at[d])
    fresh = cell[...] * (value / weight(spot.me)) / total
    next_bf[...] = fresh.astype(BF)
    next_cell[spot.me] = fresh.astype(BF)
    cell_new[...] = fresh
    fresh_sum = jnp.sum(fresh, axis=0, keepdims=True)
    next_sum[...] = fresh_sum
    next_parts[spot.me] = fresh_sum

    two = Gather(spot, next_bf, next_cell, two_sems)
    later = [d for d in range(1, far) if d != far // 2] + [far // 2]
    two.start(later)
    shared = share(spot, next_sum, next_parts, ns, nr)
    acc[...] = jnp.zeros_like(acc)

    def second_terms(chunks, j):
        total = None
        for g in chunks:
            ratio, rows_bf = ratio_of(next_cell, g, j)
            term = lax.dot_general(
                ratio, rows_bf, (((0,), (0,)), ((), ())), preferred_element_type=F32
            )
            total = term if total is None else total + term
        acc[j] += total

    def second_chunks(d, core, first, last):
        def body(e, carry):
            for j in every:
                second_terms([spot.index(spot.a_at(d), spot.b_at(e), core)], j)
            return carry

        lax.fori_loop(first, last, body, 0)

    def second_column(offsets, j):
        def body(e, carry):
            second_terms([spot.index(spot.a_at(d), spot.b_at(e), core)
                          for d in offsets for core in (0, 1)], j)
            return carry

        lax.fori_loop(0, near, body, 0)

    every = range(tiles)
    second_chunks(0, c, 0, 1)
    two.take_near(0)
    second_chunks(0, c, 1, near)
    two.ready(0)
    second_chunks(0, 1 - c, 0, near)
    for d in later:
        two.take_far(d)
    two.take_near(later[0])
    two.take_near(later[1])
    two.ready(later[0])
    second_chunks(later[0], c, 0, near)
    two.take_near(later[2])
    second_chunks(later[0], 1 - c, 0, near)
    two.ready(later[1])
    two.ready(later[2])

    mine = lax.axis_index("cell")
    for copy in shared:
        copy.wait()
    sums = jnp.sum(next_parts[...], axis=0)
    group_sum[...] = sums
    other_sum[mine] = sums
    sum_copies, copies = {}, {}
    for d in range(1, cells):
        sum_copies[d] = send(group_sum, other_sum.at[mine], os.at[d], orr.at[d],
                             {"cell": lax.rem(mine + d, cells)})

    def balance(j):
        return jnp.mean(gene_bf[j].astype(F32), axis=1, keepdims=True)

    for j in every:
        second_column(later[1:], j)
        encode(acc[j] * balance(j), code.at[j], codem.at[j])
        other[mine, j] = code[j]
        otherm[mine, j] = codem[j]
        for d in range(1, cells):
            where = {"cell": lax.rem(mine + d, cells)}
            copies[j, d] = (
                send(code.at[j], other.at[mine, j], fs.at[d, j], fr.at[d, j], where),
                send(codem.at[j], otherm.at[mine, j], uf.at[d, j], vf.at[d, j], where),
            )
    for d in range(1, cells):
        sum_copies[d].wait()
    sums = other_sum[0]
    for k in range(1, cells):
        sums += other_sum[k]
    for j in every:
        for d in range(1, cells):
            for copy in copies[j, d]:
                copy.wait()
        value = decode(other.at[0, j], otherm.at[0, j])
        for k in range(1, cells):
            value += decode(other.at[k, j], otherm.at[k, j])
        gene_new[j] = gene[j] * (value / balance(j)) / sums
    one.close()
    two.close()
    for copy in c1.values():
        copy.wait_send()
    for pair in [*c2.values(), *c3.values()]:
        for copy in pair:
            copy.wait_send()


VMEM = pl.BlockSpec(memory_space=pltpu.VMEM)
SMEM = pl.BlockSpec(memory_space=pltpu.SMEM)
ANY = pl.BlockSpec(memory_space=pl.ANY)


def step(group, cells, blocks, table, cell, gene):
    far, near, _ = digits(group)
    slots, width, _ = blocks.shape
    tiles, _, rank = gene.shape
    rows = cell.shape[0]
    dma = pltpu.SemaphoreType.DMA
    vmem = pltpu.VMEM
    return pl.pallas_call(
        functools.partial(step_kernel, group, cells),
        out_shape=(
            jax.ShapeDtypeStruct(cell.shape, F32),
            jax.ShapeDtypeStruct(gene.shape, F32),
        ),
        in_specs=[ANY, SMEM, VMEM, VMEM],
        out_specs=(VMEM, VMEM),
        scratch_shapes=[
            vmem((slots + 1, width, width), BF),
            vmem((tiles, width, rank), BF),
            vmem((tiles, rank, width), BF),
            vmem((rows, rank), BF),
            vmem((1, rank), F32),
            vmem((group, 1, rank), F32),
            vmem((group, rows, rank), BF),
            vmem((rows, rank), BF),
            vmem((1, rank), F32),
            vmem((group, 1, rank), F32),
            vmem((group, rows, rank), BF),
            vmem((group, rows, rank), F32),
            vmem((far, near, rows, rank), F32),
            vmem((far, near, rows, rank), I16),
            vmem((far, rows, rank), I16),
            vmem((far, near, rows, rank), I16),
            vmem((far, rows, rank), I16),
            vmem((far, near, 1, rank), F32),
            vmem((far, 1, rank), F32),
            vmem((far, near, 1, rank), F32),
            vmem((far, 1, rank), F32),
            vmem((tiles, width, rank), F32),
            vmem((tiles, width, rank), I16),
            vmem((tiles, 1, rank), F32),
            vmem((cells, tiles, width, rank), I16),
            vmem((cells, tiles, 1, rank), F32),
            vmem((1, rank), F32),
            vmem((cells, 1, rank), F32),
        ] + gather_sems(far, near) * 2 + [dma((far, near))] * 4 + [dma((far,))] * 2
        + [dma((group,))] * 4 + [dma((cells, tiles))] * 2 + [dma((cells,))] * 2 + [dma((1,))]
        + [dma((far, near))] * 2 + [dma((far,))] * 2 + [dma((cells, tiles))] * 2,
        compiler_params=pltpu.CompilerParams(
            collective_id=0, has_side_effects=True, vmem_limit_bytes=60 * 1024 * 1024
        ),
        name="update_step",
    )(blocks, table, cell, gene)


def on_device(cells, group, blocks, brow, bcol, bcount, cell_factor, gene_factor):
    slots, width, _ = blocks.shape
    rows, rank = cell_factor.shape
    tiles = gene_factor.shape[0] // width
    spots = jnp.arange(rows * group // width * tiles, dtype=jnp.int32)
    order = jnp.arange(slots, dtype=jnp.int32)
    where = jnp.where(order < bcount[0], brow * tiles + bcol, -1)
    table = jnp.min(jnp.where(spots[:, None] == where[None, :], order[None, :], slots), axis=1)
    cell_new, gene_new = step(group, cells, blocks, table, cell_factor,
                              gene_factor.reshape(tiles, width, rank))
    return cell_new, gene_new.reshape(gene_factor.shape)


def solution(mesh):
    sizes = dict(mesh.shape)
    placed = (
        P(("cell", "gene"), None, None),
        P(("cell", "gene")),
        P(("cell", "gene")),
        P(("cell", "gene")),
        P(("cell", "gene"), None),
        P("gene", None),
    )
    return jax.shard_map(
        functools.partial(on_device, sizes["cell"], sizes["gene"]),
        mesh=mesh,
        in_specs=placed,
        out_specs=(P(("cell", "gene"), None), P("gene", None)),
        check_vma=False,
    )
```

profile of v0, /device:TPU:0, one launch (start us, length us, event | category | flops | bytes accessed | tf_op | source)
XLA Modules:
  0.0 69.5 jit_solution(5355092207402301393)
XLA Ops:
  1.3 0.7 compare_select_fusion
  2.0 0.6 select_reduce_fusion.table
  2.6 63.5 %update_step.1 = (f32[256,128]{1,0:T(8,128)}, f32[4,256,128]{2,1,0:T(8,128)}) custom-call(bf16[48,256,256]{2,1,0:T(8,128)(2,1)} %blocks.1, s32[64]{0:T(128)} %select_reduce_fusion.table, f32[256,128]{1,0:T(8,128)} %cell.1, f32[4,256,128]{2,1,0:T(8,128)} %bitcast.5), custom_call_target="tpu_custom_call" | custom-call | tf_op jit(solution)/shard_map/update_step/pallas_call | solution.py:384
  66.0 1.6 %copy.11 = f32[256,128]{1,0:T(8,128)} copy(f32[256,128]{1,0:T(8,128)} %get-tuple-element.8) | data formatting | bytes 262144
  67.6 1.9 %copy.12 = f32[1024,128]{1,0:T(8,128)} copy(f32[1024,128]{1,0:T(8,128)} %bitcast.4) | data formatting | bytes 1048576
where the time goes:
time: 69.7 us; the launch traced here: 69.5 us
  Pallas kernels  63.5 us (91%)
  local copies, waits for them, and re-layouts  3.44 us (5%)
  between operations  1.29 us (2%)
  other arithmetic  1.28 us (2%)
    pallas_call x1, Pallas kernels, step(): pl.pallas_call(functools.partial(step_kernel, group, cells), out_shape=(j...  63.5 us
    unnamed x2, local copies, waits for them, and re-layouts  3.44 us

commit v1 on v0

v1 whole, which is shorter than its diff:
```python
import functools

import jax
import jax.numpy as jnp
from jax import lax
from jax.experimental import pallas as pl
from jax.experimental.pallas import tpu as pltpu
from jax.sharding import PartitionSpec as P

MESH = pl.DeviceIdType.MESH
F32 = jnp.float32
BF = jnp.bfloat16
I16 = jnp.int16
I32 = jnp.int32
CORES = 2
FAR = 4
PARTS = 2
LAST = 3


def digits(group):
    return FAR, group // (FAR * CORES), CORES


def flip(v, k, n):
    if k == 0:
        return v
    if k == n - 1:
        return n - 1 - v
    if k == n // 2:
        return lax.rem(v + n // 2, n)
    return v + 1 - 2 * lax.rem(v, 2)


class Spot:
    def __init__(self, group):
        self.group = group
        self.far, self.near, self.cores = digits(group)
        self.me = lax.axis_index("gene")
        self.a = self.me // (self.near * self.cores)
        self.b = lax.rem(self.me // self.cores, self.near)
        self.c = lax.rem(self.me, self.cores)

    def unit(self, k, e):
        return flip(self.a, k, self.far) * self.near + flip(self.b, e, self.near)

    def peer(self, k, e, core):
        return {"gene": self.unit(k, e) * self.cores + core}


def send(src, dst, send_sem, recv_sem, where):
    copy = pltpu.make_async_remote_copy(
        src_ref=src, dst_ref=dst, send_sem=send_sem, recv_sem=recv_sem,
        device_id=where, device_id_type=MESH,
    )
    copy.start()
    return copy


def greet(axis, size):
    barrier = pltpu.get_barrier_semaphore()
    me = lax.axis_index(axis)
    for d in range(1, size):
        pl.semaphore_signal(
            barrier, inc=1, device_id={axis: lax.rem(me + d, size)}, device_id_type=MESH
        )


def encode(value, code, scale):
    top = jnp.max(jnp.abs(value), axis=0, keepdims=True)
    factor = jnp.where(top > 0.0, 32767.0 / top, 0.0)
    code[...] = jnp.round(value * factor).astype(jnp.int32).astype(jnp.int16)
    scale[...] = top * (1.0 / 32767.0)


def decode(code, scale):
    return code[...].astype(jnp.int32).astype(F32) * scale[...]


class Gather:
    def __init__(self, spot, out, prow, sems):
        self.spot, self.out, self.prow = spot, out, prow
        self.zs, self.zr, self.xs, self.xr, self.cs, self.cr = sems
        self.zc, self.xc, self.cc = {}, {}, {}

    def place(self, h, k, e):
        spot = self.spot
        first = pl.multiple_of(spot.c * self.prow, self.prow)
        return self.out.at[h, spot.unit(k, e), pl.ds(first, self.prow)]

    def start(self, h):
        spot, src = self.spot, self.place(h, 0, 0)
        for k in range(1, spot.far):
            self.zc[h, k] = send(src, src, self.zs.at[h, k], self.zr.at[h, k],
                                 spot.peer(k, 0, spot.c))
        self.forward(h, 0)

    def forward(self, h, k):
        spot, src = self.spot, self.place(h, k, 0)
        for e in range(1, spot.near):
            self.xc[h, k, e] = send(src, src, self.xs.at[h, k, e], self.xr.at[h, k, e],
                                    spot.peer(0, e, spot.c))
        self.pair(h, k, 0)

    def pair(self, h, k, e):
        spot, src = self.spot, self.place(h, k, e)
        self.cc[h, k, e] = send(src, src, self.cs.at[h, k, e], self.cr.at[h, k, e],
                                spot.peer(0, 0, 1 - spot.c))

    def take_far(self, h, k):
        self.zc[h, k].wait_recv()
        self.forward(h, k)

    def take_near(self, h, k, e):
        self.xc[h, k, e].wait_recv()
        self.pair(h, k, e)

    def ready(self, h, k, e):
        self.cc[h, k, e].wait_recv()

    def copies(self):
        return [*self.zc.values(), *self.xc.values(), *self.cc.values()]


def gather_sems(far, near):
    dma = pltpu.SemaphoreType.DMA
    return [dma((PARTS, far))] * 2 + [dma((PARTS, far, near))] * 4


class Plan:
    def __init__(self, far, near):
        self.far, self.near = far, near
        self.time = 0.0
        self.free = {"c": 0.0, "x": 0.0, "z": 0.0}
        self.arrive = {}
        self.done = {}
        self.order = []

    def post(self, link, key, extra=0.0, weight=1.0):
        wire = {"c": 0.1, "x": 1.4, "z": 1.4}[link] / PARTS * weight
        wait = {"c": 0.9, "x": 1.9, "z": 1.9}[link]
        self.free[link] = max(self.free[link], self.time) + wire
        self.arrive[key] = self.free[link] + wait + extra

    def begin(self, name, h):
        for k in range(1, self.far):
            self.post("z", (name, "z", h, k), 0.7 * (k - 1), 2.0 if k == 3 else 1.0)
        self.ahead(name, h, 0)

    def ahead(self, name, h, k):
        for e in range(1, self.near):
            self.post("x", (name, "x", h, k, e))
        self.post("c", (name, "c", h, k, 0))

    def tasks(self):
        far, near = range(self.far), range(self.near)
        out = []
        for h in range(PARTS):
            for name in ("one", "two"):
                for k in far[1:]:
                    out.append(((name, "far", h, k), [(name, "z", h, k)], 0.02))
                for k in far:
                    for e in near[1:]:
                        out.append(((name, "near", h, k, e), [(name, "x", h, k, e)], 0.02))
            need = [("p1", h, 0, 0)] + [("p2", h, 0, e) for e in near[1:]]
            out.append((("fresh", h), need + [("p3", h, k) for k in far[1:]], 0.4))
            for k in far[1:]:
                need = [("p1", h, k, 0)] + [("p2", h, k, e) for e in near[1:]]
                out.append((("sum", h, k), need, 0.25))
            for k in far:
                for e in near[1:]:
                    out.append((("mix", h, k, e), [("p1", h, k, e)], 0.2))
        spread = [(h, k, e) for h in range(PARTS) for e in reversed(near) for k in [*far[1:], 0]]
        out += [(("first", *u), [("one", "c", *u)], 1.24 / PARTS * (self.near / 2) ** 0) for u in spread]
        out += [(("second", *u), [("two", "c", *u)], 1.24 / PARTS) for u in spread]
        return out

    def run(self, task):
        kind = task[0]
        if kind == "first":
            self.post("c", ("p1", *task[1:]))
        elif kind == "mix":
            self.post("x", ("p2", *task[1:]))
        elif kind == "sum":
            self.post("z", ("p3", *task[1:]), 0.7 * (task[2] - 1), 2.0 if task[2] == 3 else 1.0)
        elif kind == "fresh":
            self.begin("two", task[1])
        elif kind in ("one", "two") and task[1] == "far":
            self.ahead(kind, task[2], task[3])
        elif kind in ("one", "two"):
            self.post("c", (kind, "c", *task[2:]))

    def build(self):
        for h in range(PARTS):
            self.begin("one", h)
        left = self.tasks()
        while left:
            known = [(max(self.arrive[n] for n in need), i) for i, (_, need, _) in enumerate(left)
                     if all(n in self.arrive for n in need)]
            ready = [i for when, i in known if when <= self.time]
            if not ready:
                self.time = min(when for when, _ in known)
                continue
            task, _, cost = left.pop(min(ready))
            self.time += cost
            self.run(task)
            self.order.append(task)
        return self.order


def step_kernel(group, cells, blocks, brow, bcol, bcount, cell_in, gene_in, cell_new, gene_new,
                held, spread, table, cell, gene, gene_bf, flipped, own_sum, parts, cell_bf,
                next_sum, next_parts, next_cell, numer, p1, p2, p3, t2, t3,
                p2m, p3m, t2m, t3m, acc, code, codem, other, otherm, group_sum, other_sum, *sems):
    spot = Spot(group)
    far, near, cores = spot.far, spot.near, spot.cores
    c = spot.c
    slots, width, _ = blocks.shape
    tiles = gene.shape[0]
    rows = cell.shape[0]
    prow = rows // PARTS
    sub = width // rows
    one_sems, two_sems = sems[0:6], sems[6:12]
    s1, r1, s2, r2, s3, r3, gs, gr, ns, nr, fs, fr, os, orr, ls, u2, v2, u3, v3, uf, vf = sems[12:]
    greet("gene", group)
    greet("cell", cells)
    load_cell = pltpu.make_async_copy(cell_in, cell, ls.at[0])
    load_cell.start()
    load_gene = pltpu.make_async_copy(gene_in, gene, ls.at[1])
    load_gene.start()
    load = pltpu.make_async_copy(blocks, held.at[pl.ds(0, slots)], ls.at[2])
    load.start()

    lane = lax.broadcasted_iota(I32, (1, slots), 1)
    where = jnp.where(lane < bcount[0], brow[...] * tiles + bcol[...], -1)
    at = lax.broadcasted_iota(I32, (spread.shape[0], slots), 0)
    found = jnp.min(jnp.where(at == where, lane, slots), axis=1, keepdims=True)
    spread[...] = jnp.broadcast_to(found, spread.shape)
    load_table = pltpu.make_async_copy(spread, table, ls.at[3])
    load_table.start()
    held[slots] = jnp.zeros((width, width), BF)

    one = Gather(spot, cell_bf, prow, one_sems)
    two = Gather(spot, next_cell, prow, two_sems)
    load_cell.wait()
    for h in range(PARTS):
        one.place(h, 0, 0)[...] = cell[pl.ds(h * prow, prow), :].astype(BF)
    pl.semaphore_wait(pltpu.get_barrier_semaphore(), group - 1 + cells - 1)
    for h in range(PARTS):
        one.start(h)

    def share(src, out, ss, sr):
        return [
            send(src, out.at[spot.me], ss.at[d], sr.at[d], {"gene": lax.rem(spot.me + d, group)})
            for d in range(1, group)
        ]

    load_gene.wait()
    first_sum = jnp.zeros((1, gene.shape[-1]), F32)
    for j in range(tiles):
        first_sum += jnp.sum(gene[j], axis=0, keepdims=True)
    own_sum[...] = first_sum
    parts[spot.me] = first_sum
    shared = share(own_sum, parts, gs, gr)
    for j in range(tiles):
        gene_bf[j] = gene[j].astype(BF)
        flipped[j] = gene[j].astype(BF).T
    acc[...] = jnp.zeros_like(acc)
    load_table.wait()
    load.wait()

    def ratio_of(source, h, u, j):
        rows_bf = source[h, u]
        found = []
        for core in range(cores):
            g = u * cores + core
            slot = table[(g // sub) * tiles + j, 0]
            if sub == 1:
                found.append(held[slot, pl.ds(h * prow, prow), :])
            else:
                first = pl.multiple_of(lax.rem(g, sub) * rows + h * prow, prow)
                found.append(held[slot, pl.ds(first, prow), :])
        x = jnp.concatenate(found, axis=0)
        model = jnp.dot(rows_bf, flipped[j], preferred_element_type=F32)
        return (x.astype(F32) / model).astype(BF), rows_bf

    c1, c2, c3 = {}, {}, {}
    mine_at = pl.ds(pl.multiple_of(c * prow, prow), prow)
    theirs_at = pl.ds(pl.multiple_of((1 - c) * prow, prow), prow)

    def first(h, k, e):
        one.ready(h, k, e)
        u = spot.unit(k, e)
        total = None
        for j in range(tiles):
            ratio, _ = ratio_of(cell_bf, h, u, j)
            term = jnp.dot(ratio, gene_bf[j], preferred_element_type=F32)
            total = term if total is None else total + term
        numer[h, u] = total
        c1[h, k, e] = send(numer.at[h, u, theirs_at], p1.at[h, k, e], s1.at[h, k, e],
                           r1.at[h, k, e], spot.peer(0, 0, 1 - c))

    def weight(h, u):
        return jnp.mean(cell_bf[h, u, mine_at].astype(F32), axis=1, keepdims=True)

    def both(h, k, e):
        c1[h, k, e].wait_recv()
        u = spot.unit(k, e)
        return (numer[h, u, mine_at] + p1[h, k, e]) * weight(h, u)

    def mix(h, k, e):
        encode(both(h, k, e), t2.at[h, k, e], t2m.at[h, k, e])
        where = spot.peer(0, e, c)
        c2[h, k, e] = (
            send(t2.at[h, k, e], p2.at[h, k, e], s2.at[h, k, e], r2.at[h, k, e], where),
            send(t2m.at[h, k, e], p2m.at[h, k, e], u2.at[h, k, e], v2.at[h, k, e], where),
        )

    def summed(h, k):
        value = both(h, k, 0)
        for e in range(1, near):
            for copy in c2[h, k, e]:
                copy.wait_recv()
            value += decode(p2.at[h, k, e], p2m.at[h, k, e])
        return value

    def stage_sum(h, k):
        encode(summed(h, k), t3.at[h, k], t3m.at[h, k])
        where = spot.peer(k, 0, c)
        c3[h, k] = (
            send(t3.at[h, k], p3.at[h, k], s3.at[h, k], r3.at[h, k], where),
            send(t3m.at[h, k], p3m.at[h, k], u3.at[h, k], v3.at[h, k], where),
        )

    sums_of = {}

    def fresh(h):
        if "total" not in sums_of:
            for copy in shared:
                copy.wait()
            sums_of["total"] = jnp.sum(parts[...], axis=0)
        value = summed(h, 0)
        for k in range(1, far):
            for copy in c3[h, k]:
                copy.wait_recv()
            value += decode(p3.at[h, k], p3m.at[h, k])
        value = value / weight(h, spot.unit(0, 0))
        new = cell[pl.ds(h * prow, prow), :] * value / sums_of["total"]
        two.place(h, 0, 0)[...] = new.astype(BF)
        two.start(h)
        cell_new[pl.ds(h * prow, prow), :] = new
        sums_of[h] = jnp.sum(new, axis=0, keepdims=True)
        if all(i in sums_of for i in range(PARTS)):
            total = sums_of[0]
            for i in range(1, PARTS):
                total = total + sums_of[i]
            next_sum[...] = total
            next_parts[spot.me] = total
            sums_of["shared"] = share(next_sum, next_parts, ns, nr)

    def second(units, j):
        total = acc[j]
        for h, k, e in units:
            ratio, rows_bf = ratio_of(next_cell, h, spot.unit(k, e), j)
            total = total + lax.dot_general(
                ratio, rows_bf, (((0,), (0,)), ((), ())), preferred_element_type=F32
            )
        acc[j] = total

    order = Plan(far, near).build()
    seconds = [task[1:] for task in order if task[0] == "second"]
    late = seconds[-LAST:]
    for task in order:
        kind = task[0]
        if kind in ("one", "two"):
            side = one if kind == "one" else two
            if task[1] == "far":
                side.take_far(*task[2:])
            else:
                side.take_near(*task[2:])
        elif kind == "first":
            first(*task[1:])
        elif kind == "mix":
            mix(*task[1:])
        elif kind == "sum":
            stage_sum(*task[1:])
        elif kind == "fresh":
            fresh(*task[1:])
        elif task[1:] not in late:
            two.ready(*task[1:])
            for j in range(tiles):
                second([task[1:]], j)
    for task in late:
        two.ready(*task)

    def balance(j):
        return jnp.mean(gene_bf[j].astype(F32), axis=1, keepdims=True)

    mine = lax.axis_index("cell")
    sum_copies, copies = {}, {}
    for j in range(tiles):
        second(late, j)
        encode(acc[j] * balance(j), code.at[j], codem.at[j])
        for d in range(1, cells):
            where = {"cell": lax.rem(mine + d, cells)}
            copies[j, d] = (
                send(code.at[j], other.at[mine, j], fs.at[d, j], fr.at[d, j], where),
                send(codem.at[j], otherm.at[mine, j], uf.at[d, j], vf.at[d, j], where),
            )
        other[mine, j] = code[j]
        otherm[mine, j] = codem[j]
        if j == 0:
            for copy in sums_of["shared"]:
                copy.wait()
            sums = jnp.sum(next_parts[...], axis=0)
            group_sum[...] = sums
            other_sum[mine] = sums
            for d in range(1, cells):
                sum_copies[d] = send(group_sum, other_sum.at[mine], os.at[d], orr.at[d],
                                     {"cell": lax.rem(mine + d, cells)})
    for d in range(1, cells):
        sum_copies[d].wait()
    sums = other_sum[0]
    for k in range(1, cells):
        sums += other_sum[k]
    for j in range(tiles):
        for d in range(1, cells):
            for copy in copies[j, d]:
                copy.wait()
        value = decode(other.at[0, j], otherm.at[0, j])
        for k in range(1, cells):
            value += decode(other.at[k, j], otherm.at[k, j])
        gene_new[j] = gene[j] * (value / balance(j)) / sums
    for copy in [*one.copies(), *two.copies(), *c1.values()]:
        copy.wait_send()
    for pair in [*c2.values(), *c3.values()]:
        for copy in pair:
            copy.wait_send()


VMEM = pl.BlockSpec(memory_space=pltpu.VMEM)
SMEM = pl.BlockSpec(memory_space=pltpu.SMEM)
ANY = pl.BlockSpec(memory_space=pl.ANY)


def step(group, cells, blocks, brow, bcol, bcount, cell, gene):
    far, near, cores = digits(group)
    slots, width, _ = blocks.shape
    tiles, _, rank = gene.shape
    rows = cell.shape[0]
    prow = rows // PARTS
    spots = rows * group // width * tiles
    dma = pltpu.SemaphoreType.DMA
    vmem = pltpu.VMEM
    hke = (PARTS, far, near)
    return pl.pallas_call(
        functools.partial(step_kernel, group, cells),
        out_shape=(vmem(cell.shape, F32), vmem(gene.shape, F32)),
        in_specs=[ANY, VMEM, VMEM, SMEM, ANY, ANY],
        out_specs=(VMEM, VMEM),
        scratch_shapes=[
            vmem((slots + 1, width, width), BF),
            vmem((spots, 128), I32),
            pltpu.SMEM((spots, 128), I32),
            vmem((rows, rank), F32),
            vmem((tiles, width, rank), F32),
            vmem((tiles, width, rank), BF),
            vmem((tiles, rank, width), BF),
            vmem((1, rank), F32),
            vmem((group, 1, rank), F32),
            vmem((PARTS, far * near, cores * prow, rank), BF),
            vmem((1, rank), F32),
            vmem((group, 1, rank), F32),
            vmem((PARTS, far * near, cores * prow, rank), BF),
            vmem((PARTS, far * near, cores * prow, rank), F32),
            vmem((*hke, prow, rank), F32),
            vmem((*hke, prow, rank), I16),
            vmem((PARTS, far, prow, rank), I16),
            vmem((*hke, prow, rank), I16),
            vmem((PARTS, far, prow, rank), I16),
            vmem((*hke, 1, rank), F32),
            vmem((PARTS, far, 1, rank), F32),
            vmem((*hke, 1, rank), F32),
            vmem((PARTS, far, 1, rank), F32),
            vmem((tiles, width, rank), F32),
            vmem((tiles, width, rank), I16),
            vmem((tiles, 1, rank), F32),
            vmem((cells, tiles, width, rank), I16),
            vmem((cells, tiles, 1, rank), F32),
            vmem((1, rank), F32),
            vmem((cells, 1, rank), F32),
        ] + gather_sems(far, near) * 2 + [dma(hke)] * 4 + [dma((PARTS, far))] * 2
        + [dma((group,))] * 4 + [dma((cells, tiles))] * 2 + [dma((cells,))] * 2 + [dma((4,))]
        + [dma(hke)] * 2 + [dma((PARTS, far))] * 2 + [dma((cells, tiles))] * 2,
        compiler_params=pltpu.CompilerParams(
            collective_id=0, has_side_effects=True, vmem_limit_bytes=60 * 1024 * 1024
        ),
        name="update_step",
    )(blocks, brow, bcol, bcount, cell, gene)


def on_device(cells, group, blocks, brow, bcol, bcount, cell_factor, gene_factor):
    _, width, _ = blocks.shape
    rank = cell_factor.shape[-1]
    tiles = gene_factor.shape[0] // width
    cell_new, gene_new = step(group, cells, blocks, brow.reshape(1, -1), bcol.reshape(1, -1), bcount,
                              cell_factor, gene_factor.reshape(tiles, width, rank))
    return cell_new, gene_new.reshape(gene_factor.shape)


def solution(mesh):
    sizes = dict(mesh.shape)
    placed = (
        P(("cell", "gene"), None, None),
        P(("cell", "gene")),
        P(("cell", "gene")),
        P(("cell", "gene")),
        P(("cell", "gene"), None),
        P("gene", None),
    )
    return jax.shard_map(
        functools.partial(on_device, sizes["cell"], sizes["gene"]),
        mesh=mesh,
        in_specs=placed,
        out_specs=(P(("cell", "gene"), None), P("gene", None)),
        check_vma=False,
    )
```

time: 69.7 us -> 56.6 us (0.81)
  Pallas kernels: 63.5 us -> 53.6 us
  local copies, waits for them, and re-layouts: 3.44 us -> 1.45 us
  other arithmetic: 1.28 us -> 0 us
    pallas_call x1, Pallas kernels: 63.5 us -> 53.6 us  [step(): pl.pallas_call(functools.partial(step_kernel, group, cells), out_shape=(v...]
    unnamed x2, local copies, waits for them, and re-layouts: 3.44 us -> 1.45 us
where the time goes in v1:
time: 56.6 us; the launch traced here: 56.4 us
  Pallas kernels  53.6 us (95%)
  local copies, waits for them, and re-layouts  1.45 us (3%)
  between operations  1.29 us (2%)
    pallas_call x1, Pallas kernels, step(): pl.pallas_call(functools.partial(step_kernel, group, cells), out_shape=(v...  53.6 us
    unnamed x2, local copies, waits for them, and re-layouts  1.45 us

profile of v1, /device:TPU:0, one launch (start us, length us, event | category | flops | bytes accessed | tf_op | source)
XLA Modules:
  0.0 56.4 jit_solution(8248933786870605017)
XLA Ops:
  1.3 53.6 %update_step.1 = (f32[256,128]{1,0:T(8,128)S(1)}, f32[4,256,128]{2,1,0:T(8,128)S(1)}) custom-call(bf16[48,256,256]{2,1,0:T(8,128)(2,1)} %blocks.1, s32[1,48]{1,0:T(1,128)} %bitcast.6, s32[1,48]{1,0:T(1,128)} %bitcast.7, s32[1]{0:T(128)S(6)} %copy.12.bcount, f32[256,128]{1,0:T(8,128)} %cell_in.1, f32[4,256,128]{2,1,0:T(8,128)} %bitcast.5), custom_call_target="tpu_custom_call" | custom-call | tf_op jit(solution)/shard_map/update_step/pallas_call | solution.py:456
  54.9 0.7 %copy.10 = f32[256,128]{1,0:T(8,128)} copy(f32[256,128]{1,0:T(8,128)S(1)} %get-tuple-element.6) | data formatting | bytes 262144
  55.6 0.8 %copy.11 = f32[1024,128]{1,0:T(8,128)} copy(f32[1024,128]{1,0:T(8,128)S(1)} %bitcast.4) | data formatting | bytes 1048576

commit v2 on v1

v2 whole, which is shorter than its diff:
```python
import functools

import jax
import jax.numpy as jnp
from jax import lax
from jax.experimental import pallas as pl
from jax.experimental.pallas import tpu as pltpu
from jax.sharding import PartitionSpec as P

MESH = pl.DeviceIdType.MESH
F32 = jnp.float32
BF = jnp.bfloat16
I16 = jnp.int16
I32 = jnp.int32
CORES = 2
FAR = 4
PARTS = 2
LAST = 2
AHEAD = (1, 2, 3)
SPREAD = (3, 2, 1, 0)
PATIENCE = 0.0
COST = {"first": (1.24, 1.64), "second": (1.28, 1.8)}
WAIT = {"c": 0.95, "x": 2.2, "near": 2.6, "mid": 1.5}


def digits(group):
    return FAR, group // (FAR * CORES), CORES


def flip(v, k, n):
    if k == 0:
        return v
    if k == n - 1:
        return n - 1 - v
    if k == n // 2:
        return lax.rem(v + n // 2, n)
    return v + 1 - 2 * lax.rem(v, 2)


class Spot:
    def __init__(self, group):
        self.group = group
        self.far, self.near, self.cores = digits(group)
        self.me = lax.axis_index("gene")
        self.a = self.me // (self.near * self.cores)
        self.b = lax.rem(self.me // self.cores, self.near)
        self.c = lax.rem(self.me, self.cores)

    def unit(self, k, e):
        return flip(self.a, k, self.far) * self.near + flip(self.b, e, self.near)

    def peer(self, k, e, core):
        return {"gene": self.unit(k, e) * self.cores + core}


def send(src, dst, send_sem, recv_sem, where):
    copy = pltpu.make_async_remote_copy(
        src_ref=src, dst_ref=dst, send_sem=send_sem, recv_sem=recv_sem,
        device_id=where, device_id_type=MESH,
    )
    copy.start()
    return copy


def drain(ref, sem):
    pltpu.make_async_copy(ref, ref, sem).wait()


def greet(axis, size):
    barrier = pltpu.get_barrier_semaphore()
    me = lax.axis_index(axis)
    for d in range(1, size):
        pl.semaphore_signal(
            barrier, inc=1, device_id={axis: lax.rem(me + d, size)}, device_id_type=MESH
        )


def encode(value, code, scale):
    top = jnp.max(jnp.abs(value), axis=0, keepdims=True)
    factor = jnp.where(top > 0.0, 32767.0 / top, 0.0)
    code[...] = jnp.round(value * factor).astype(jnp.int32).astype(jnp.int16)
    scale[...] = top * (1.0 / 32767.0)


def decode(code, scale):
    return code[...].astype(jnp.int32).astype(F32) * scale[...]


class Gather:
    def __init__(self, spot, out, prow, sems):
        self.spot, self.out, self.prow = spot, out, prow
        self.sent, self.zr, self.xr, self.cr = sems
        self.zc, self.xc, self.cc = {}, {}, {}

    def place(self, h, k, e):
        spot = self.spot
        first = pl.multiple_of(spot.c * self.prow, self.prow)
        return self.out.at[h, spot.unit(k, e), pl.ds(first, self.prow)]

    def start(self, h):
        spot, src = self.spot, self.place(h, 0, 0)
        for k in AHEAD:
            self.zc[h, k] = send(src, src, self.sent.at[0], self.zr.at[h, k - 1],
                                 spot.peer(k, 0, spot.c))
        self.forward(h, 0)

    def forward(self, h, k):
        spot, src = self.spot, self.place(h, k, 0)
        for e in range(1, spot.near):
            self.xc[h, k, e] = send(src, src, self.sent.at[1], self.xr.at[h, k, e - 1],
                                    spot.peer(0, e, spot.c))
        self.pair(h, k, 0)

    def pair(self, h, k, e):
        spot, src = self.spot, self.place(h, k, e)
        self.cc[h, k, e] = send(src, src, self.sent.at[2], self.cr.at[h, k, e],
                                spot.peer(0, 0, 1 - spot.c))

    def take_far(self, h, k):
        self.zc[h, k].wait_recv()
        self.forward(h, k)

    def take_near(self, h, k, e):
        self.xc[h, k, e].wait_recv()
        self.pair(h, k, e)

    def ready(self, h, k, e):
        self.cc[h, k, e].wait_recv()

    def close(self):
        far, near = self.spot.far, self.spot.near
        for i, units in enumerate((far - 1, far * (near - 1), far * near)):
            drain(self.out.at[0, pl.ds(0, units)], self.sent.at[i])


def gather_sems(far, near):
    dma = pltpu.SemaphoreType.DMA
    return [dma((3,)), dma((PARTS, far - 1)), dma((PARTS, far, near - 1)), dma((PARTS, far, near))]


class Plan:
    def __init__(self, far, near):
        self.far, self.near = far, near
        self.time = 0.0
        self.free = {"c": 0.0, "x": 0.0, "near": 0.0, "mid": 0.0}
        self.arrive = {}
        self.order = []

    def post(self, key, k, e):
        link = "x" if e else ("c", "near", "mid", "mid")[k]
        wire = {"c": 0.1, "x": 1.4, "near": 1.4, "mid": 2.8}[link] / PARTS
        self.free[link] = max(self.time, self.free[link]) + wire
        self.arrive[key] = self.free[link] + WAIT[link]

    def begin(self, name, h):
        for k in AHEAD:
            self.post((name, "z", h, k), k, 0)
        self.ahead(name, h, 0)

    def ahead(self, name, h, k):
        for e in range(1, self.near):
            self.post((name, "x", h, k, e), 0, e)
        self.post((name, "c", h, k, 0), 0, 0)

    def tasks(self):
        far, near, parts = range(self.far), range(self.near), range(PARTS)
        mixed = [("p2", h, k, e) for h in parts for k in far for e in near[1:]]
        out = []
        for h in parts:
            out += [((name, "far", h, k), [(name, "z", h, k)], 0.02)
                    for name in ("one", "two") for k in far[1:]]
        for h in parts:
            need = [("p1", h, 0, 0)] + [("p3", h, k) for k in far[1:]]
            need += [key for key in mixed if key[1] == h and key[2] == 0]
            out.append((("fresh", h), need, 0.35))
        for h in parts:
            for k in reversed(far[1:]):
                need = [("p1", h, k, 0)]
                need += [key for key in mixed if key[1:3] == (h, k)]
                out.append((("sum", h, k), need, 0.15))
        for h in parts:
            out += [(("mix", h, k, e), [("p1", h, k, e)], 0.14)
                    for k in reversed(far) for e in near[1:]]
        for h in parts:
            out += [((name, "near", h, k, e), [(name, "x", h, k, e)], 0.02)
                    for name in ("one", "two") for k in far for e in near[1:]]
        spread = [(h, k, e) for h in parts for e in reversed(near) for k in SPREAD]
        for name, side in (("first", "one"), ("second", "two")):
            out += [((name, u), [(side, "c", *u)], COST[name][0] / PARTS) for u in spread]
        return out

    def run(self, task):
        kind = task[0]
        if kind == "first":
            for unit in task[1:]:
                self.post(("p1", *unit), 0, 0)
        elif kind == "mix":
            h, k, e = task[1:]
            self.post(("p2", h, k, e), 0, e)
        elif kind == "sum":
            self.post(("p3", *task[1:]), task[2], 0)
        elif kind == "fresh":
            self.begin("two", task[1])
        elif kind in ("one", "two") and task[1] == "far":
            self.ahead(kind, task[2], task[3])
        elif kind in ("one", "two"):
            self.post((kind, "c", *task[2:]), 0, 0)

    def build(self):
        for h in range(PARTS):
            self.begin("one", h)
        self.time = 0.5
        left = self.tasks()
        while left:
            known = [(max(self.arrive[n] for n in need), i) for i, (_, need, _) in enumerate(left)
                     if all(n in self.arrive for n in need)]
            ready = [i for when, i in known if when <= self.time]
            if not ready:
                self.time = min(when for when, _ in known)
                continue
            pick = min(ready)
            kind = left[pick][0][0]
            if kind in COST:
                alike = sorted((max(when, self.time), i) for when, i in known
                               if left[i][0][0] == kind and i != pick)
                soon = [when for when, _ in known if when > self.time]
                if alike and alike[0][0] > self.time and min(soon) <= self.time + PATIENCE:
                    self.time = min(soon)
                    continue
                if alike and alike[0][0] <= self.time:
                    other = alike[0][1]
                    units = left[pick][0][1:] + left[other][0][1:]
                    for i in sorted((pick, other), reverse=True):
                        left.pop(i)
                    left.insert(0, ((kind, *units), [], COST[kind][1] / PARTS))
                    pick = 0
            task, _, cost = left.pop(pick)
            self.time += cost
            self.run(task)
            self.order.append(task)
        return self.order


def step_kernel(group, cells, blocks, brow_in, bcol_in, bcount_in, cell_in, gene_in, cell_new,
                gene_new, brow, bcol, bcount, held, spread, table, cell, gene, gene_bf, flipped, own_sum, parts, cell_bf,
                next_sum, next_parts, next_cell, numer, p1, p2, p3, t2, t3,
                p2m, p3m, t2m, t3m, acc, code, codem, other, otherm, group_sum, other_sum, *sems):
    spot = Spot(group)
    far, near, cores = spot.far, spot.near, spot.cores
    c = spot.c
    slots, width, _ = blocks.shape
    tiles = gene.shape[0]
    rows = cell.shape[0]
    prow = rows // PARTS
    sub = width // rows
    one_sems, two_sems = sems[0:4], sems[4:8]
    sent, r1, r2, v2, r3, v3, gr, nr, fr, vf, orr, ls = sems[8:]
    s1, s2, u2, s3, u3, gs, ns, fs, uf, os = (sent.at[i] for i in range(10))
    greet("gene", group)
    greet("cell", cells)
    load_cell = pltpu.make_async_copy(cell_in, cell, ls.at[0])
    load_cell.start()
    small = [pltpu.make_async_copy(src, dst, ls.at[4 + i])
             for i, (src, dst) in enumerate(((brow_in, brow), (bcol_in, bcol), (bcount_in, bcount)))]
    for copy in small:
        copy.start()
    load_gene = pltpu.make_async_copy(gene_in, gene, ls.at[1])
    load_gene.start()
    load = pltpu.make_async_copy(blocks, held.at[pl.ds(0, slots)], ls.at[2])
    load.start()

    held[slots] = jnp.zeros((width, width), BF)
    for copy in small:
        copy.wait()
    lane = lax.broadcasted_iota(I32, (1, slots), 1)
    where = jnp.where(lane < bcount[0], brow[...] * tiles + bcol[...], -1)
    at = lax.broadcasted_iota(I32, (spread.shape[0], slots), 0)
    found = jnp.min(jnp.where(at == where, lane, slots), axis=1, keepdims=True)
    spread[...] = jnp.broadcast_to(found, spread.shape)
    load_table = pltpu.make_async_copy(spread, table, ls.at[3])
    load_table.start()

    one = Gather(spot, cell_bf, prow, one_sems)
    two = Gather(spot, next_cell, prow, two_sems)
    load_cell.wait()
    for h in range(PARTS):
        one.place(h, 0, 0)[...] = cell[pl.ds(h * prow, prow), :].astype(BF)
    pl.semaphore_wait(pltpu.get_barrier_semaphore(), group - 1 + cells - 1)
    for h in range(PARTS):
        one.start(h)

    def share(src, out, ss, sr):
        for d in range(1, group):
            send(src, out.at[spot.me], ss, sr.at[0], {"gene": lax.rem(spot.me + d, group)})

    load_gene.wait()
    first_sum = jnp.zeros((1, gene.shape[-1]), F32)
    for j in range(tiles):
        first_sum += jnp.sum(gene[j], axis=0, keepdims=True)
    own_sum[...] = first_sum
    parts[spot.me] = first_sum
    share(own_sum, parts, gs, gr)
    for j in range(tiles):
        gene_bf[j] = gene[j].astype(BF)
        flipped[j] = gene[j].astype(BF).T
    acc[...] = jnp.zeros_like(acc)
    load_table.wait()
    load.wait()

    def rows_of(source, units):
        return jnp.concatenate([source[h, spot.unit(k, e)] for h, k, e in units], axis=0)

    def ratio_of(rows_bf, units, j):
        found = []
        for h, k, e in units:
            for core in range(cores):
                g = spot.unit(k, e) * cores + core
                slot = table[(g // sub) * tiles + j, 0]
                if sub == 1:
                    found.append(held[slot, pl.ds(h * prow, prow), :])
                else:
                    first = pl.multiple_of(lax.rem(g, sub) * rows + h * prow, prow)
                    found.append(held[slot, pl.ds(first, prow), :])
        x = jnp.concatenate(found, axis=0)
        model = jnp.dot(rows_bf, flipped[j], preferred_element_type=F32)
        return (x.astype(F32) / model).astype(BF)

    c1, c2, c3 = {}, {}, {}
    mine_at = pl.ds(pl.multiple_of(c * prow, prow), prow)
    theirs_at = pl.ds(pl.multiple_of((1 - c) * prow, prow), prow)

    def first(*units):
        for unit in units:
            one.ready(*unit)
        rows_bf = rows_of(cell_bf, units)
        total = None
        for j in range(tiles):
            ratio = ratio_of(rows_bf, units, j)
            term = jnp.dot(ratio, gene_bf[j], preferred_element_type=F32)
            total = term if total is None else total + term
        for i, (h, k, e) in enumerate(units):
            u = spot.unit(k, e)
            numer[h, u] = total[i * cores * prow:(i + 1) * cores * prow]
            c1[h, k, e] = send(numer.at[h, u, theirs_at], p1.at[h, k, e], s1,
                               r1.at[h, k, e], spot.peer(0, 0, 1 - c))

    def weight(h, u):
        return jnp.mean(cell_bf[h, u, mine_at].astype(F32), axis=1, keepdims=True)

    def both(h, k, e):
        c1[h, k, e].wait_recv()
        u = spot.unit(k, e)
        return (numer[h, u, mine_at] + p1[h, k, e]) * weight(h, u)

    def mix(h, k, e):
        encode(both(h, k, e), t2.at[h, k, e], t2m.at[h, k, e])
        where = spot.peer(0, e, c)
        c2[h, k, e] = (
            send(t2.at[h, k, e], p2.at[h, k, e], s2, r2.at[h, k, e - 1], where),
            send(t2m.at[h, k, e], p2m.at[h, k, e], u2, v2.at[h, k, e - 1], where),
        )

    def summed(h, k):
        value = both(h, k, 0)
        for e in range(1, near):
            for copy in c2[h, k, e]:
                copy.wait_recv()
            value += decode(p2.at[h, k, e], p2m.at[h, k, e])
        return value

    def stage_sum(h, k):
        encode(summed(h, k), t3.at[h, k], t3m.at[h, k])
        where = spot.peer(k, 0, c)
        c3[h, k] = (
            send(t3.at[h, k], p3.at[h, k], s3, r3.at[h, k - 1], where),
            send(t3m.at[h, k], p3m.at[h, k], u3, v3.at[h, k - 1], where),
        )

    sums_of = {}

    def fresh(h):
        if "total" not in sums_of:
            drain(parts.at[pl.ds(0, group - 1)], gr.at[0])
            sums_of["total"] = jnp.sum(parts[...], axis=0)
        value = summed(h, 0)
        for k in range(1, far):
            for copy in c3[h, k]:
                copy.wait_recv()
            value += decode(p3.at[h, k], p3m.at[h, k])
        value = value / weight(h, spot.unit(0, 0))
        new = cell[pl.ds(h * prow, prow), :] * value / sums_of["total"]
        two.place(h, 0, 0)[...] = new.astype(BF)
        two.start(h)
        cell_new[pl.ds(h * prow, prow), :] = new
        sums_of[h] = jnp.sum(new, axis=0, keepdims=True)
        if all(i in sums_of for i in range(PARTS)):
            total = sums_of[0]
            for i in range(1, PARTS):
                total = total + sums_of[i]
            next_sum[...] = total
            next_parts[spot.me] = total
            share(next_sum, next_parts, ns, nr)

    def second(units, rows_bf, j):
        ratio = ratio_of(rows_bf, units, j)
        acc[j] += lax.dot_general(
            ratio, rows_bf, (((0,), (0,)), ((), ())), preferred_element_type=F32
        )

    order = Plan(far, near).build()
    late = [unit for task in order if task[0] == "second" for unit in task[1:]][-LAST:]
    for task in order:
        kind = task[0]
        if kind in ("one", "two"):
            side = one if kind == "one" else two
            if task[1] == "far":
                side.take_far(*task[2:])
            else:
                side.take_near(*task[2:])
        elif kind == "first":
            first(*task[1:])
        elif kind == "mix":
            mix(*task[1:])
        elif kind == "sum":
            stage_sum(*task[1:])
        elif kind == "fresh":
            fresh(*task[1:])
        else:
            units = [unit for unit in task[1:] if unit not in late]
            for unit in units:
                two.ready(*unit)
            rows_bf = rows_of(next_cell, units) if units else None
            for j in range(tiles if units else 0):
                second(units, rows_bf, j)
    for unit in late:
        two.ready(*unit)
    late_rows = rows_of(next_cell, late)

    def balance(j):
        return jnp.mean(gene_bf[j].astype(F32), axis=1, keepdims=True)

    mine = lax.axis_index("cell")
    sum_copies, copies = {}, {}
    for j in range(tiles):
        second(late, late_rows, j)
        encode(acc[j] * balance(j), code.at[j], codem.at[j])
        for d in range(1, cells):
            where = {"cell": lax.rem(mine + d, cells)}
            copies[j, d] = (
                send(code.at[j], other.at[mine, j], fs, fr.at[d - 1, j], where),
                send(codem.at[j], otherm.at[mine, j], uf, vf.at[d - 1, j], where),
            )
        other[mine, j] = code[j]
        otherm[mine, j] = codem[j]
        if j == 0:
            drain(next_parts.at[pl.ds(0, group - 1)], nr.at[0])
            sums = jnp.sum(next_parts[...], axis=0)
            group_sum[...] = sums
            other_sum[mine] = sums
            for d in range(1, cells):
                sum_copies[d] = send(group_sum, other_sum.at[mine], os, orr.at[d - 1],
                                     {"cell": lax.rem(mine + d, cells)})
    for d in range(1, cells):
        sum_copies[d].wait_recv()
    sums = other_sum[0]
    for k in range(1, cells):
        sums += other_sum[k]
    for j in range(tiles):
        for d in range(1, cells):
            for copy in copies[j, d]:
                copy.wait_recv()
        value = decode(other.at[0, j], otherm.at[0, j])
        for k in range(1, cells):
            value += decode(other.at[k, j], otherm.at[k, j])
        gene_new[j] = gene[j] * (value / balance(j)) / sums
    one.close()
    two.close()
    drain(numer.at[0], s1)
    drain(t2.at[:, :, 0:near - 1], s2)
    drain(t2m.at[:, :, 0:near - 1], u2)
    drain(t3.at[:, 1:far], s3)
    drain(t3m.at[:, 1:far], u3)
    drain(parts.at[pl.ds(0, group - 1)], gs)
    drain(next_parts.at[pl.ds(0, group - 1)], ns)
    drain(other.at[0:cells - 1], fs)
    drain(otherm.at[0:cells - 1], uf)
    drain(other_sum.at[0:cells - 1], os)


VMEM = pl.BlockSpec(memory_space=pltpu.VMEM)
HBM = pl.BlockSpec(memory_space=pltpu.HBM)


def step(group, cells, blocks, brow, bcol, bcount, cell, gene):
    far, near, cores = digits(group)
    slots, width, _ = blocks.shape
    tiles, _, rank = gene.shape
    rows = cell.shape[0]
    prow = rows // PARTS
    spots = rows * group // width * tiles
    dma = pltpu.SemaphoreType.DMA
    vmem = pltpu.VMEM
    hke = (PARTS, far, near)
    return pl.pallas_call(
        functools.partial(step_kernel, group, cells),
        out_shape=(vmem(cell.shape, F32), vmem(gene.shape, F32)),
        in_specs=[HBM] * 6,
        out_specs=(VMEM, VMEM),
        scratch_shapes=[
            vmem((1, slots), I32),
            vmem((1, slots), I32),
            pltpu.SMEM((1,), I32),
            vmem((slots + 1, width, width), BF),
            vmem((spots, 128), I32),
            pltpu.SMEM((spots, 128), I32),
            vmem((rows, rank), F32),
            vmem((tiles, width, rank), F32),
            vmem((tiles, width, rank), BF),
            vmem((tiles, rank, width), BF),
            vmem((1, rank), F32),
            vmem((group, 1, rank), F32),
            vmem((PARTS, far * near, cores * prow, rank), BF),
            vmem((1, rank), F32),
            vmem((group, 1, rank), F32),
            vmem((PARTS, far * near, cores * prow, rank), BF),
            vmem((PARTS, far * near, cores * prow, rank), F32),
            vmem((*hke, prow, rank), F32),
            vmem((*hke, prow, rank), I16),
            vmem((PARTS, far, prow, rank), I16),
            vmem((*hke, prow, rank), I16),
            vmem((PARTS, far, prow, rank), I16),
            vmem((*hke, 1, rank), F32),
            vmem((PARTS, far, 1, rank), F32),
            vmem((*hke, 1, rank), F32),
            vmem((PARTS, far, 1, rank), F32),
            vmem((tiles, width, rank), F32),
            vmem((tiles, width, rank), I16),
            vmem((tiles, 1, rank), F32),
            vmem((cells, tiles, width, rank), I16),
            vmem((cells, tiles, 1, rank), F32),
            vmem((1, rank), F32),
            vmem((cells, 1, rank), F32),
        ] + gather_sems(far, near) * 2 + [dma((10,)), dma(hke)]
        + [dma((PARTS, far, near - 1))] * 2 + [dma((PARTS, far - 1))] * 2 + [dma((1,))] * 2
        + [dma((cells - 1, tiles))] * 2 + [dma((cells - 1,)), dma((7,))],
        compiler_params=pltpu.CompilerParams(
            collective_id=0, has_side_effects=True, vmem_limit_bytes=60 * 1024 * 1024
        ),
        name="update_step",
    )(blocks, brow, bcol, bcount, cell, gene)


def on_device(cells, group, blocks, brow, bcol, bcount, cell_factor, gene_factor):
    _, width, _ = blocks.shape
    rank = cell_factor.shape[-1]
    tiles = gene_factor.shape[0] // width
    cell_new, gene_new = step(group, cells, blocks, brow.reshape(1, -1), bcol.reshape(1, -1), bcount,
                              cell_factor, gene_factor.reshape(tiles, width, rank))
    return cell_new, gene_new.reshape(gene_factor.shape)


def solution(mesh):
    sizes = dict(mesh.shape)
    placed = (
        P(("cell", "gene"), None, None),
        P(("cell", "gene")),
        P(("cell", "gene")),
        P(("cell", "gene")),
        P(("cell", "gene"), None),
        P("gene", None),
    )
    return jax.shard_map(
        functools.partial(on_device, sizes["cell"], sizes["gene"]),
        mesh=mesh,
        in_specs=placed,
        out_specs=(P(("cell", "gene"), None), P("gene", None)),
        check_vma=False,
    )
```

time: 56.6 us -> 53 us (0.936)
  Pallas kernels: 53.6 us -> 50.1 us
    pallas_call x1, Pallas kernels: 53.6 us -> 50.1 us  [step(): pl.pallas_call(functools.partial(step_kernel, group, cells), out_shape=(v...]
where the time goes in v2:
time: 53 us; the launch traced here: 52.9 us
  Pallas kernels  50.1 us (95%)
  local copies, waits for them, and re-layouts  1.45 us (3%)
  between operations  1.29 us (2%)
    pallas_call x1, Pallas kernels, step(): pl.pallas_call(functools.partial(step_kernel, group, cells), out_shape=(v...  50.1 us
    unnamed x2, local copies, waits for them, and re-layouts  1.45 us

profile of v2, /device:TPU:0, one launch (start us, length us, event | category | flops | bytes accessed | tf_op | source)
XLA Modules:
  0.0 52.9 jit_solution(6606643458910169721)
XLA Ops:
  1.3 50.1 %update_step.1 = (f32[256,128]{1,0:T(8,128)S(1)}, f32[4,256,128]{2,1,0:T(8,128)S(1)}) custom-call(bf16[48,256,256]{2,1,0:T(8,128)(2,1)} %blocks.1, s32[1,48]{1,0:T(1,128)} %bitcast.6, s32[1,48]{1,0:T(1,128)} %bitcast.7, s32[1]{0:T(128)S(6)} %copy.12.bcount_in, f32[256,128]{1,0:T(8,128)} %cell_in.1, f32[4,256,128]{2,1,0:T(8,128)} %bitcast.5), custom_call_target="tpu_custom_call" | custom-call | tf_op jit(solution)/shard_map/update_step/pallas_call | solution.py:504
  51.4 0.7 %copy.10 = f32[256,128]{1,0:T(8,128)} copy(f32[256,128]{1,0:T(8,128)S(1)} %get-tuple-element.6) | data formatting | bytes 262144
  52.1 0.8 %copy.11 = f32[1024,128]{1,0:T(8,128)} copy(f32[1024,128]{1,0:T(8,128)S(1)} %bitcast.4) | data formatting | bytes 1048576

commit v3 on v2

--- a/solution.py
+++ b/solution.py
@@ -17,6 +17,7 @@
 PARTS = 2
 LAST = 2
 AHEAD = (1, 2, 3)
+DIRECT = {"one": (), "sum": (), "two": ((0, 1), (1, 1))}
 SPREAD = (3, 2, 1, 0)
 PATIENCE = 0.0
 COST = {"first": (1.24, 1.64), "second": (1.28, 1.8)}
@@ -87,7 +88,8 @@
 
 
 class Gather:
-    def __init__(self, spot, out, prow, sems):
+    def __init__(self, spot, out, prow, direct, sems):
+        self.direct = direct
         self.spot, self.out, self.prow = spot, out, prow
         self.sent, self.zr, self.xr, self.cr = sems
         self.zc, self.xc, self.cc = {}, {}, {}
@@ -103,10 +105,14 @@
             self.zc[h, k] = send(src, src, self.sent.at[0], self.zr.at[h, k - 1],
                                  spot.peer(k, 0, spot.c))
         self.forward(h, 0)
+        for k in AHEAD:
+            for e in range(1, spot.near if (h, k) in self.direct else 1):
+                self.xc[h, k, e] = send(src, src, self.sent.at[1], self.xr.at[h, k, e - 1],
+                                        spot.peer(k, e, spot.c))
 
     def forward(self, h, k):
         spot, src = self.spot, self.place(h, k, 0)
-        for e in range(1, spot.near):
+        for e in range(1, 1 if (h, k) in self.direct else spot.near):
             self.xc[h, k, e] = send(src, src, self.sent.at[1], self.xr.at[h, k, e - 1],
                                     spot.peer(0, e, spot.c))
         self.pair(h, k, 0)
@@ -147,18 +153,21 @@
         self.order = []
 
     def post(self, key, k, e):
-        link = "x" if e else ("c", "near", "mid", "mid")[k]
+        link = ("x" if e else "c", "near", "mid", "mid")[k]
         wire = {"c": 0.1, "x": 1.4, "near": 1.4, "mid": 2.8}[link] / PARTS
         self.free[link] = max(self.time, self.free[link]) + wire
-        self.arrive[key] = self.free[link] + WAIT[link]
+        self.arrive[key] = self.free[link] + WAIT[link] + (0.7 if k and e else 0.0)
 
     def begin(self, name, h):
         for k in AHEAD:
             self.post((name, "z", h, k), k, 0)
         self.ahead(name, h, 0)
+        for k in AHEAD:
+            for e in range(1, self.near if (h, k) in DIRECT[name] else 1):
+                self.post((name, "x", h, k, e), k, e)
 
     def ahead(self, name, h, k):
-        for e in range(1, self.near):
+        for e in range(1, 1 if (h, k) in DIRECT[name] else self.near):
             self.post((name, "x", h, k, e), 0, e)
         self.post((name, "c", h, k, 0), 0, 0)
 
@@ -171,12 +180,12 @@
                     for name in ("one", "two") for k in far[1:]]
         for h in parts:
             need = [("p1", h, 0, 0)] + [("p3", h, k) for k in far[1:]]
-            need += [key for key in mixed if key[1] == h and key[2] == 0]
+            need += [key for key in mixed if key[1] == h and (key[2] == 0 or (h, key[2]) in DIRECT["sum"])]
             out.append((("fresh", h), need, 0.35))
         for h in parts:
             for k in reversed(far[1:]):
                 need = [("p1", h, k, 0)]
-                need += [key for key in mixed if key[1:3] == (h, k)]
+                need += [key for key in mixed if key[1:3] == (h, k) and (h, k) not in DIRECT["sum"]]
                 out.append((("sum", h, k), need, 0.15))
         for h in parts:
             out += [(("mix", h, k, e), [("p1", h, k, e)], 0.14)
@@ -196,7 +205,7 @@
                 self.post(("p1", *unit), 0, 0)
         elif kind == "mix":
             h, k, e = task[1:]
-            self.post(("p2", h, k, e), 0, e)
+            self.post(("p2", h, k, e), k if (h, k) in DIRECT["sum"] else 0, e)
         elif kind == "sum":
             self.post(("p3", *task[1:]), task[2], 0)
         elif kind == "fresh":
@@ -244,7 +253,7 @@
 def step_kernel(group, cells, blocks, brow_in, bcol_in, bcount_in, cell_in, gene_in, cell_new,
                 gene_new, brow, bcol, bcount, held, spread, table, cell, gene, gene_bf, flipped, own_sum, parts, cell_bf,
                 next_sum, next_parts, next_cell, numer, p1, p2, p3, t2, t3,
-                p2m, p3m, t2m, t3m, acc, code, codem, other, otherm, group_sum, other_sum, *sems):
+                p2m, p3m, t2m, t3m, acc, code, codem, other, otherm, group_sum, other_sum, size, *sems):
     spot = Spot(group)
     far, near, cores = spot.far, spot.near, spot.cores
     c = spot.c
@@ -253,8 +262,8 @@
     rows = cell.shape[0]
     prow = rows // PARTS
     sub = width // rows
-    one_sems, two_sems = sems[0:4], sems[4:8]
-    sent, r1, r2, v2, r3, v3, gr, nr, fr, vf, orr, ls = sems[8:]
+    one_sems, two_sems = sems[0:4], [sems[4], *sems[1:4]]
+    sent, r1, r2, r3, gr, nr, fr, orr, ls = sems[5:]
     s1, s2, u2, s3, u3, gs, ns, fs, uf, os = (sent.at[i] for i in range(10))
     greet("gene", group)
     greet("cell", cells)
@@ -280,8 +289,8 @@
     load_table = pltpu.make_async_copy(spread, table, ls.at[3])
     load_table.start()
 
-    one = Gather(spot, cell_bf, prow, one_sems)
-    two = Gather(spot, next_cell, prow, two_sems)
+    one = Gather(spot, cell_bf, prow, DIRECT["one"], one_sems)
+    two = Gather(spot, next_cell, prow, DIRECT["two"], two_sems)
     load_cell.wait()
     for h in range(PARTS):
         one.place(h, 0, 0)[...] = cell[pl.ds(h * prow, prow), :].astype(BF)
@@ -325,7 +334,7 @@
         model = jnp.dot(rows_bf, flipped[j], preferred_element_type=F32)
         return (x.astype(F32) / model).astype(BF)
 
-    c1, c2, c3 = {}, {}, {}
+    c1 = {}
     mine_at = pl.ds(pl.multiple_of(c * prow, prow), prow)
     theirs_at = pl.ds(pl.multiple_of((1 - c) * prow, prow), prow)
 
@@ -354,27 +363,23 @@
 
     def mix(h, k, e):
         encode(both(h, k, e), t2.at[h, k, e], t2m.at[h, k, e])
-        where = spot.peer(0, e, c)
-        c2[h, k, e] = (
-            send(t2.at[h, k, e], p2.at[h, k, e], s2, r2.at[h, k, e - 1], where),
-            send(t2m.at[h, k, e], p2m.at[h, k, e], u2, v2.at[h, k, e - 1], where),
-        )
-
-    def summed(h, k):
+        where = spot.peer(k if (h, k) in DIRECT["sum"] else 0, e, c)
+        send(t2.at[h, k, e], p2.at[h, k, e], s2, r2.at[h, k, e - 1], where)
+        send(t2m.at[h, k, e], p2m.at[h, k, e], u2, r2.at[h, k, e - 1], where)
+
+    def summed(h, k, mixed):
         value = both(h, k, 0)
-        for e in range(1, near):
-            for copy in c2[h, k, e]:
-                copy.wait_recv()
-            value += decode(p2.at[h, k, e], p2m.at[h, k, e])
+        for i in mixed:
+            for e in range(1, near):
+                drain(size.at[pl.ds(0, prow // 2 + 1)], r2.at[h, i, e - 1])
+                value += decode(p2.at[h, i, e], p2m.at[h, i, e])
         return value
 
     def stage_sum(h, k):
-        encode(summed(h, k), t3.at[h, k], t3m.at[h, k])
+        encode(summed(h, k, () if (h, k) in DIRECT["sum"] else (k,)), t3.at[h, k], t3m.at[h, k])
         where = spot.peer(k, 0, c)
-        c3[h, k] = (
-            send(t3.at[h, k], p3.at[h, k], s3, r3.at[h, k - 1], where),
-            send(t3m.at[h, k], p3m.at[h, k], u3, v3.at[h, k - 1], where),
-        )
+        send(t3.at[h, k], p3.at[h, k], s3, r3.at[h, k - 1], where)
+        send(t3m.at[h, k], p3m.at[h, k], u3, r3.at[h, k - 1], where)
 
     sums_of = {}
 
@@ -382,10 +387,9 @@
         if "total" not in sums_of:
             drain(parts.at[pl.ds(0, group - 1)], gr.at[0])
             sums_of["total"] = jnp.sum(parts[...], axis=0)
-        value = summed(h, 0)
+        value = summed(h, 0, [k for k in range(far) if k == 0 or (h, k) in DIRECT["sum"]])
         for k in range(1, far):
-            for copy in c3[h, k]:
-                copy.wait_recv()
+            drain(size.at[pl.ds(0, prow // 2 + 1)], r3.at[h, k - 1])
             value += decode(p3.at[h, k], p3m.at[h, k])
         value = value / weight(h, spot.unit(0, 0))
         new = cell[pl.ds(h * prow, prow), :] * value / sums_of["total"]
@@ -440,16 +444,14 @@
         return jnp.mean(gene_bf[j].astype(F32), axis=1, keepdims=True)
 
     mine = lax.axis_index("cell")
-    sum_copies, copies = {}, {}
+    sum_copies = {}
     for j in range(tiles):
         second(late, late_rows, j)
         encode(acc[j] * balance(j), code.at[j], codem.at[j])
         for d in range(1, cells):
             where = {"cell": lax.rem(mine + d, cells)}
-            copies[j, d] = (
-                send(code.at[j], other.at[mine, j], fs, fr.at[d - 1, j], where),
-                send(codem.at[j], otherm.at[mine, j], uf, vf.at[d - 1, j], where),
-            )
+            send(code.at[j], other.at[mine, j], fs, fr.at[d - 1, j], where)
+            send(codem.at[j], otherm.at[mine, j], uf, fr.at[d - 1, j], where)
         other[mine, j] = code[j]
         otherm[mine, j] = codem[j]
         if j == 0:
@@ -467,8 +469,7 @@
         sums += other_sum[k]
     for j in range(tiles):
         for d in range(1, cells):
-            for copy in copies[j, d]:
-                copy.wait_recv()
+            drain(size.at[pl.ds(0, width // 2 + 1)], fr.at[d - 1, j])
         value = decode(other.at[0, j], otherm.at[0, j])
         for k in range(1, cells):
             value += decode(other.at[k, j], otherm.at[k, j])
@@ -540,9 +541,10 @@
             vmem((cells, tiles, 1, rank), F32),
             vmem((1, rank), F32),
             vmem((cells, 1, rank), F32),
-        ] + gather_sems(far, near) * 2 + [dma((10,)), dma(hke)]
-        + [dma((PARTS, far, near - 1))] * 2 + [dma((PARTS, far - 1))] * 2 + [dma((1,))] * 2
-        + [dma((cells - 1, tiles))] * 2 + [dma((cells - 1,)), dma((7,))],
+            vmem((width // 2 + 1, 1, rank), F32),
+        ] + gather_sems(far, near) + [dma((3,)), dma((10,)), dma(hke)]
+        + [dma((PARTS, far, near - 1)), dma((PARTS, far - 1))] + [dma((1,))] * 2
+        + [dma((cells - 1, tiles)), dma((cells - 1,)), dma((7,))],
         compiler_params=pltpu.CompilerParams(
             collective_id=0, has_side_effects=True, vmem_limit_bytes=60 * 1024 * 1024
         ),

time: 53 us -> 51.7 us (0.975)
  Pallas kernels: 50.1 us -> 48.8 us
    pallas_call x1, Pallas kernels: 50.1 us -> 48.8 us  [step(): pl.pallas_call(functools.partial(step_kernel, group, cells), out_shape=(v...]
where the time goes in v3:
time: 51.7 us; the launch traced here: 51.6 us
  Pallas kernels  48.8 us (94%)
  local copies, waits for them, and re-layouts  1.45 us (3%)
  between operations  1.29 us (2%)
    pallas_call x1, Pallas kernels, step(): pl.pallas_call(functools.partial(step_kernel, group, cells), out_shape=(v...  48.8 us
    unnamed x2, local copies, waits for them, and re-layouts  1.45 us

profile of v3, /device:TPU:0, one launch (start us, length us, event | category | flops | bytes accessed | tf_op | source)
XLA Modules:
  0.0 51.6 jit_solution(1798087102780600760)
XLA Ops:
  1.3 48.8 %update_step.1 = (f32[256,128]{1,0:T(8,128)S(1)}, f32[4,256,128]{2,1,0:T(8,128)S(1)}) custom-call(bf16[48,256,256]{2,1,0:T(8,128)(2,1)} %blocks.1, s32[1,48]{1,0:T(1,128)} %bitcast.6, s32[1,48]{1,0:T(1,128)} %bitcast.7, s32[1]{0:T(128)S(6)} %copy.12.bcount_in, f32[256,128]{1,0:T(8,128)} %cell_in.1, f32[4,256,128]{2,1,0:T(8,128)} %bitcast.5), custom_call_target="tpu_custom_call" | custom-call | tf_op jit(solution)/shard_map/update_step/pallas_call | solution.py:505
  50.1 0.7 %copy.10 = f32[256,128]{1,0:T(8,128)} copy(f32[256,128]{1,0:T(8,128)S(1)} %get-tuple-element.6) | data formatting | bytes 262144
  50.8 0.8 %copy.11 = f32[1024,128]{1,0:T(8,128)} copy(f32[1024,128]{1,0:T(8,128)S(1)} %bitcast.4) | data formatting | bytes 1048576

commit v4 on v3

--- a/solution.py
+++ b/solution.py
@@ -19,9 +19,9 @@
 AHEAD = (1, 2, 3)
 DIRECT = {"one": (), "sum": (), "two": ((0, 1), (1, 1))}
 SPREAD = (3, 2, 1, 0)
-PATIENCE = 0.0
+PAIR = 0.5
 COST = {"first": (1.24, 1.64), "second": (1.28, 1.8)}
-WAIT = {"c": 0.95, "x": 2.2, "near": 2.6, "mid": 1.5}
+WAIT = {"c": 0.95, "x": 1.8, "near": 2.6, "mid": 1.5}
 
 
 def digits(group):
@@ -232,11 +232,8 @@
             if kind in COST:
                 alike = sorted((max(when, self.time), i) for when, i in known
                                if left[i][0][0] == kind and i != pick)
-                soon = [when for when, _ in known if when > self.time]
-                if alike and alike[0][0] > self.time and min(soon) <= self.time + PATIENCE:
-                    self.time = min(soon)
-                    continue
-                if alike and alike[0][0] <= self.time:
+                if alike and alike[0][0] <= self.time + PAIR:
+                    self.time = alike[0][0]
                     other = alike[0][1]
                     units = left[pick][0][1:] + left[other][0][1:]
                     for i in sorted((pick, other), reverse=True):

time: 51.7 us -> 50.9 us (0.985)
  Pallas kernels: 48.8 us -> 48 us
    pallas_call x1, Pallas kernels: 48.8 us -> 48 us  [step(): pl.pallas_call(functools.partial(step_kernel, group, cells), out_shape=(v...]
where the time goes in v4:
time: 50.9 us; the launch traced here: 50.8 us
  Pallas kernels  48 us (94%)
  local copies, waits for them, and re-layouts  1.45 us (3%)
  between operations  1.29 us (3%)
    pallas_call x1, Pallas kernels, step(): pl.pallas_call(functools.partial(step_kernel, group, cells), out_shape=(v...  48 us
    unnamed x2, local copies, waits for them, and re-layouts  1.45 us

profile of v4, /device:TPU:0, one launch (start us, length us, event | category | flops | bytes accessed | tf_op | source)
XLA Modules:
  0.0 50.8 jit_solution(8507179256516888839)
XLA Ops:
  1.3 48.0 %update_step.1 = (f32[256,128]{1,0:T(8,128)S(1)}, f32[4,256,128]{2,1,0:T(8,128)S(1)}) custom-call(bf16[48,256,256]{2,1,0:T(8,128)(2,1)} %blocks.1, s32[1,48]{1,0:T(1,128)} %bitcast.6, s32[1,48]{1,0:T(1,128)} %bitcast.7, s32[1]{0:T(128)S(6)} %copy.12.bcount_in, f32[256,128]{1,0:T(8,128)} %cell_in.1, f32[4,256,128]{2,1,0:T(8,128)} %bitcast.5), custom_call_target="tpu_custom_call" | custom-call | tf_op jit(solution)/shard_map/update_step/pallas_call | solution.py:502
  49.3 0.7 %copy.10 = f32[256,128]{1,0:T(8,128)} copy(f32[256,128]{1,0:T(8,128)S(1)} %get-tuple-element.6) | data formatting | bytes 262144
  50.0 0.8 %copy.11 = f32[1024,128]{1,0:T(8,128)} copy(f32[1024,128]{1,0:T(8,128)S(1)} %bitcast.4) | data formatting | bytes 1048576

commit v5 on v4

--- a/solution.py
+++ b/solution.py
@@ -18,7 +18,7 @@
 LAST = 2
 AHEAD = (1, 2, 3)
 DIRECT = {"one": (), "sum": (), "two": ((0, 1), (1, 1))}
-SPREAD = (3, 2, 1, 0)
+SPREAD = (3, 2, 0, 1)
 PAIR = 0.5
 COST = {"first": (1.24, 1.64), "second": (1.28, 1.8)}
 WAIT = {"c": 0.95, "x": 1.8, "near": 2.6, "mid": 1.5}
@@ -101,10 +101,10 @@
 
     def start(self, h):
         spot, src = self.spot, self.place(h, 0, 0)
+        self.forward(h, 0)
         for k in AHEAD:
             self.zc[h, k] = send(src, src, self.sent.at[0], self.zr.at[h, k - 1],
                                  spot.peer(k, 0, spot.c))
-        self.forward(h, 0)
         for k in AHEAD:
             for e in range(1, spot.near if (h, k) in self.direct else 1):
                 self.xc[h, k, e] = send(src, src, self.sent.at[1], self.xr.at[h, k, e - 1],
@@ -250,7 +250,7 @@
 def step_kernel(group, cells, blocks, brow_in, bcol_in, bcount_in, cell_in, gene_in, cell_new,
                 gene_new, brow, bcol, bcount, held, spread, table, cell, gene, gene_bf, flipped, own_sum, parts, cell_bf,
                 next_sum, next_parts, next_cell, numer, p1, p2, p3, t2, t3,
-                p2m, p3m, t2m, t3m, acc, code, codem, other, otherm, group_sum, other_sum, size, *sems):
+                p2m, p3m, t2m, t3m, acc, code, codem, other, otherm, group_sum, other_sum, size, even, *sems):
     spot = Spot(group)
     far, near, cores = spot.far, spot.near, spot.cores
     c = spot.c
@@ -275,6 +275,15 @@
     load = pltpu.make_async_copy(blocks, held.at[pl.ds(0, slots)], ls.at[2])
     load.start()
 
+    one = Gather(spot, cell_bf, prow, DIRECT["one"], one_sems)
+    two = Gather(spot, next_cell, prow, DIRECT["two"], two_sems)
+    load_cell.wait()
+    for h in range(PARTS):
+        one.place(h, 0, 0)[...] = cell[pl.ds(h * prow, prow), :].astype(BF)
+    pl.semaphore_wait(pltpu.get_barrier_semaphore(), group - 1 + cells - 1)
+    for h in range(PARTS):
+        one.start(h)
+
     held[slots] = jnp.zeros((width, width), BF)
     for copy in small:
         copy.wait()
@@ -286,15 +295,6 @@
     load_table = pltpu.make_async_copy(spread, table, ls.at[3])
     load_table.start()
 
-    one = Gather(spot, cell_bf, prow, DIRECT["one"], one_sems)
-    two = Gather(spot, next_cell, prow, DIRECT["two"], two_sems)
-    load_cell.wait()
-    for h in range(PARTS):
-        one.place(h, 0, 0)[...] = cell[pl.ds(h * prow, prow), :].astype(BF)
-    pl.semaphore_wait(pltpu.get_barrier_semaphore(), group - 1 + cells - 1)
-    for h in range(PARTS):
-        one.start(h)
-
     def share(src, out, ss, sr):
         for d in range(1, group):
             send(src, out.at[spot.me], ss, sr.at[0], {"gene": lax.rem(spot.me + d, group)})
@@ -309,6 +309,8 @@
     for j in range(tiles):
         gene_bf[j] = gene[j].astype(BF)
         flipped[j] = gene[j].astype(BF).T
+        mean = jnp.mean(gene[j].astype(BF).astype(F32), axis=1, keepdims=True)
+        even[j] = jnp.broadcast_to(mean, even.shape[1:])
     acc[...] = jnp.zeros_like(acc)
     load_table.wait()
     load.wait()
@@ -438,7 +440,7 @@
     late_rows = rows_of(next_cell, late)
 
     def balance(j):
-        return jnp.mean(gene_bf[j].astype(F32), axis=1, keepdims=True)
+        return even[j]
 
     mine = lax.axis_index("cell")
     sum_copies = {}
@@ -470,7 +472,7 @@
         value = decode(other.at[0, j], otherm.at[0, j])
         for k in range(1, cells):
             value += decode(other.at[k, j], otherm.at[k, j])
-        gene_new[j] = gene[j] * (value / balance(j)) / sums
+        gene_new[j] = gene[j] * (value / even[j]) / sums
     one.close()
     two.close()
     drain(numer.at[0], s1)
@@ -539,6 +541,7 @@
             vmem((1, rank), F32),
             vmem((cells, 1, rank), F32),
             vmem((width // 2 + 1, 1, rank), F32),
+            vmem((tiles, width, rank), F32),
         ] + gather_sems(far, near) + [dma((3,)), dma((10,)), dma(hke)]
         + [dma((PARTS, far, near - 1)), dma((PARTS, far - 1))] + [dma((1,))] * 2
         + [dma((cells - 1, tiles)), dma((cells - 1,)), dma((7,))],

time: 50.9 us -> 50.8 us (level)
  no operation moved by 1% of the time
where the time goes in v5:
time: 50.8 us; the launch traced here: 50.7 us
  Pallas kernels  48 us (94%)
  local copies, waits for them, and re-layouts  1.45 us (3%)
  between operations  1.29 us (3%)
    pallas_call x1, Pallas kernels, step(): pl.pallas_call(functools.partial(step_kernel, group, cells), out_shape=(v...  48 us
    unnamed x2, local copies, waits for them, and re-layouts  1.45 us

profile of v5, /device:TPU:0, one launch (start us, length us, event | category | flops | bytes accessed | tf_op | source)
XLA Modules:
  0.0 50.7 jit_solution(7920272037912397741)
XLA Ops:
  1.3 48.0 %update_step.1 = (f32[256,128]{1,0:T(8,128)S(1)}, f32[4,256,128]{2,1,0:T(8,128)S(1)}) custom-call(bf16[48,256,256]{2,1,0:T(8,128)(2,1)} %blocks.1, s32[1,48]{1,0:T(1,128)} %bitcast.6, s32[1,48]{1,0:T(1,128)} %bitcast.7, s32[1]{0:T(128)S(6)} %copy.12.bcount_in, f32[256,128]{1,0:T(8,128)} %cell_in.1, f32[4,256,128]{2,1,0:T(8,128)} %bitcast.5), custom_call_target="tpu_custom_call" | custom-call | tf_op jit(solution)/shard_map/update_step/pallas_call | solution.py:504
  49.2 0.7 %copy.10 = f32[256,128]{1,0:T(8,128)} copy(f32[256,128]{1,0:T(8,128)S(1)} %get-tuple-element.6) | data formatting | bytes 262144
  49.9 0.8 %copy.11 = f32[1024,128]{1,0:T(8,128)} copy(f32[1024,128]{1,0:T(8,128)S(1)} %bitcast.4) | data formatting | bytes 1048576

commit v6 on v5

--- a/solution.py
+++ b/solution.py
@@ -18,7 +18,7 @@
 LAST = 2
 AHEAD = (1, 2, 3)
 DIRECT = {"one": (), "sum": (), "two": ((0, 1), (1, 1))}
-SPREAD = (3, 2, 0, 1)
+SPREAD = (2, 3, 1, 0)
 PAIR = 0.5
 COST = {"first": (1.24, 1.64), "second": (1.28, 1.8)}
 WAIT = {"c": 0.95, "x": 1.8, "near": 2.6, "mid": 1.5}

time: 50.8 us -> 50.8 us (level)
  no operation moved by 1% of the time
where the time goes in v6:
time: 50.8 us; the launch traced here: 50.7 us
  Pallas kernels  48 us (94%)
  local copies, waits for them, and re-layouts  1.45 us (3%)
  between operations  1.29 us (3%)
    pallas_call x1, Pallas kernels, step(): pl.pallas_call(functools.partial(step_kernel, group, cells), out_shape=(v...  48 us
    unnamed x2, local copies, waits for them, and re-layouts  1.45 us

profile of v6, /device:TPU:0, one launch (start us, length us, event | category | flops | bytes accessed | tf_op | source)
XLA Modules:
  0.0 50.7 jit_solution(7920272037912397741)
XLA Ops:
  1.3 48.0 %update_step.1 = (f32[256,128]{1,0:T(8,128)S(1)}, f32[4,256,128]{2,1,0:T(8,128)S(1)}) custom-call(bf16[48,256,256]{2,1,0:T(8,128)(2,1)} %blocks.1, s32[1,48]{1,0:T(1,128)} %bitcast.6, s32[1,48]{1,0:T(1,128)} %bitcast.7, s32[1]{0:T(128)S(6)} %copy.12.bcount_in, f32[256,128]{1,0:T(8,128)} %cell_in.1, f32[4,256,128]{2,1,0:T(8,128)} %bitcast.5), custom_call_target="tpu_custom_call" | custom-call | tf_op jit(solution)/shard_map/update_step/pallas_call | solution.py:504
  49.2 0.7 %copy.10 = f32[256,128]{1,0:T(8,128)} copy(f32[256,128]{1,0:T(8,128)S(1)} %get-tuple-element.6) | data formatting | bytes 262144
  49.9 0.8 %copy.11 = f32[1024,128]{1,0:T(8,128)} copy(f32[1024,128]{1,0:T(8,128)S(1)} %bitcast.4) | data formatting | bytes 1048576
